TPU v7x, 32 devices: a whole 2x2x4 slice. The times are simulated.
32 devices in a mesh: dp: 4 (over y, core), ctx: 4 (over z), tsp: 2 (over x).
Axes of the slice: x: 2, y: 2, z: 4, core: 2. Of those that a mesh axis runs over, the one named last changes fastest.
Arguments:
- grad_out: bfloat16 [4, 1024, 8192], P('dp', 'ctx', 'tsp'), may hold values from -6 to 6
- attn_out: bfloat16 [4, 1024, 4096], P('dp', None, 'ctx'), may hold values from -6 to 6
- out_weight: bfloat16 [4096, 8192], P('ctx', 'tsp'), may hold values from -0.0625 to 0.0625
- query: bfloat16 [4, 1024, 4096], P('dp', 'tsp', 'ctx'), may hold values from -128 to 128
- keys: bfloat16 [4, 1024, 512], P('dp'), may hold values from -128 to 128
- values: bfloat16 [4, 1024, 512], P('dp'), may hold values from -6 to 6
- segment_ids: int32 [4, 1024], P('dp'), may hold values from 0 to 7, never falling along the last dimension, each value on 1 to 256 neighbouring positions
- tile_live: int32 [4, 8, 8], P('dp'), may hold values 0 or 1
Outputs:
- grad_query: bfloat16 [4, 1024, 4096], P('dp', 'tsp', 'ctx')
- grad_keys: bfloat16 [4, 1024, 512], P('dp', ('ctx', 'tsp'))
- grad_values: bfloat16 [4, 1024, 512], P('dp', ('ctx', 'tsp'))
- grad_weight: float32 [4096, 8192], P('ctx', 'tsp')
Inputs may be any that keep to these rules, and one draw needn't show every extreme that they name: `segment_ids`: segment numbers never fall along a row and segment 0 is the source document; each segment has 1 to 256 tokens, one exactly that many.
All inputs are finite; a program needn't handle non-finite values. No bound on the sum of `tile_live` on one device may be relied on, other than what follows from the above.
Results may differ from a plain program's by a relative error of at most 0.0058.
Values may be sent and summed in bfloat16 or wider, within the bound.
A program may use at most 128 MiB of HBM per device.

v0:
```python
import math
import jax
import jax.numpy as jnp
from jax import lax
from jax.sharding import PartitionSpec as P

HEADS = 32
KV_HEADS = 4
HEAD_DIM = 128
TILE = 128


def merge_group(tensor_in):
    row_count = tensor_in.shape[0]
    folded = tensor_in.reshape(row_count, KV_HEADS, HEADS // KV_HEADS, HEAD_DIM).sum(axis=2)
    return folded.reshape(row_count, KV_HEADS * HEAD_DIM)


def per_device(grad_out, attn_out, out_weight, query, keys, values, segment_ids, tile_live):
    score_scale = 1.0 / math.sqrt(HEAD_DIM)
    out_all = attn_out[0]
    seq_len = out_all.shape[0]
    feat_width = out_all.shape[1]
    dy_block = lax.all_gather(grad_out, "ctx", axis=1, tiled=True)[0]
    proj_rows = lax.dot_general(
        dy_block, out_weight, (((1,), (1,)), ((), ())), preferred_element_type=jnp.float32
    )
    grad_part = proj_rows
    weight_part = lax.dot_general(
        out_all, dy_block, (((0,), (0,)), ((), ())), preferred_element_type=jnp.float32
    )
    grad_part, weight_part = (grad_part, weight_part)
    weight_quarter = lax.psum_scatter(
        weight_part.astype(jnp.bfloat16), "dp", scatter_dimension=0, tiled=True
    )
    grad_weight = lax.all_gather(weight_quarter, "dp", axis=0, tiled=True).astype(jnp.float32)
    out_grad = lax.psum_scatter(grad_part, "tsp", scatter_dimension=0, tiled=True).astype(
        jnp.bfloat16
    )
    quarter = out_grad.shape[0]
    row_start = lax.axis_index("tsp") * quarter
    heads_dev = feat_width // HEAD_DIM
    group_size = HEADS // KV_HEADS
    head_ids = lax.axis_index("ctx") * heads_dev + jnp.arange(heads_dev, dtype=jnp.int32)
    kv_ids = head_ids // group_size
    query_pos = row_start + jnp.arange(quarter, dtype=jnp.int32)
    key_pos = jnp.arange(seq_len, dtype=jnp.int32)
    tile_count = seq_len // TILE
    tile_rows = lax.dynamic_slice_in_dim(tile_live[0], row_start // TILE, quarter // TILE, 0)
    tile_mask = (
        jnp.broadcast_to(
            tile_rows[:, None, :, None], (quarter // TILE, TILE, tile_count, TILE)
        ).reshape(quarter, seq_len)
        == 1
    )
    same_tile = query_pos[:, None] // TILE == key_pos[None, :] // TILE
    segments = segment_ids[0]
    query_seg = lax.dynamic_slice_in_dim(segments, row_start, quarter, 0)
    same_doc = (segments[None, :] == query_seg[:, None]) | (segments[None, :] == 0)
    allowed = (tile_mask | same_tile) & same_doc & (key_pos[None, :] <= query_pos[:, None])
    query_heads = query[0].reshape(quarter, heads_dev, HEAD_DIM)
    grad_heads = out_grad.reshape(quarter, heads_dev, HEAD_DIM)
    output_heads = lax.dynamic_slice_in_dim(out_all, row_start, quarter, 0).reshape(
        quarter, heads_dev, HEAD_DIM
    )
    key_heads = jnp.take(keys[0].reshape(seq_len, KV_HEADS, HEAD_DIM), kv_ids, axis=1)
    value_heads = jnp.take(values[0].reshape(seq_len, KV_HEADS, HEAD_DIM), kv_ids, axis=1)
    scores = (
        jnp.einsum("qhd,khd->hqk", query_heads, key_heads, preferred_element_type=jnp.float32)
        * score_scale
    )
    scores = jnp.where(allowed[None], scores, -jnp.inf)
    row_max = jnp.max(scores, axis=2, keepdims=True)
    lse = row_max + jnp.log(jnp.sum(jnp.exp(scores - row_max), axis=2, keepdims=True))
    probs_f = jnp.where(allowed[None], jnp.exp(scores - lse), 0.0)
    probs = probs_f.astype(jnp.bfloat16)
    value_terms = jnp.einsum("hqk,qhd->hkd", probs, grad_heads, preferred_element_type=jnp.float32)
    dprobs = jnp.einsum("qhd,khd->hqk", grad_heads, value_heads, preferred_element_type=jnp.float32)
    delta = jnp.sum(grad_heads.astype(jnp.float32) * output_heads.astype(jnp.float32), axis=2).T[
        :, :, None
    ]
    dscores = (probs_f * (dprobs - delta)).astype(jnp.bfloat16)
    grad_query = (
        (
            jnp.einsum("hqk,khd->qhd", dscores, key_heads, preferred_element_type=jnp.float32)
            * score_scale
        )
        .astype(jnp.bfloat16)
        .reshape(quarter, feat_width)
    )
    key_terms = (
        jnp.einsum("hqk,qhd->hkd", dscores, query_heads, preferred_element_type=jnp.float32)
        * score_scale
    )
    local_groups = max(1, heads_dev // group_size)

    def fold_local(terms):
        folded = terms.reshape(local_groups, heads_dev // local_groups, seq_len, HEAD_DIM).sum(
            axis=1
        )
        return folded.transpose(1, 0, 2).reshape(seq_len, local_groups * HEAD_DIM)

    def fold_remote(recv):
        spread = recv.shape[1] // (KV_HEADS * HEAD_DIM)
        folded = recv.reshape(recv.shape[0], KV_HEADS, spread, HEAD_DIM).sum(axis=2)
        return folded.reshape(recv.shape[0], KV_HEADS * HEAD_DIM)

    key_recv = lax.all_to_all(fold_local(key_terms), "ctx", split_axis=0, concat_axis=1, tiled=True)
    value_recv = lax.all_to_all(
        fold_local(value_terms), "ctx", split_axis=0, concat_axis=1, tiled=True
    )
    key_part = lax.psum_scatter(fold_remote(key_recv), "tsp", scatter_dimension=0, tiled=True)
    value_part = lax.psum_scatter(fold_remote(value_recv), "tsp", scatter_dimension=0, tiled=True)
    grad_keys = key_part.astype(jnp.bfloat16)[None]
    grad_values = value_part.astype(jnp.bfloat16)[None]
    return (grad_query[None], grad_keys, grad_values, grad_weight)


def solution(mesh):
    placed = (
        P("dp", "ctx", "tsp"),
        P("dp", None, "ctx"),
        P("ctx", "tsp"),
        P("dp", "tsp", "ctx"),
        P("dp", None, None),
        P("dp", None, None),
        P("dp", None),
        P("dp", None, None),
    )
    return jax.shard_map(
        per_device,
        mesh=mesh,
        in_specs=placed,
        out_specs=(
            P("dp", "tsp", "ctx"),
            P("dp", ("ctx", "tsp"), None),
            P("dp", ("ctx", "tsp"), None),
            P("ctx", "tsp"),
        ),
        check_vma=False,
    )
```

profile of v0, /device:TPU:0, one launch (start us, length us, event | category | flops | bytes accessed | tf_op | source)
XLA Modules:
  0.0 416.2 jit_solution(13732216424792096202)
XLA Ops:
  8.0 154.0 %all-gather.3.cloned.1.call-done = bf16[1,1024,4096]{2,1,0:T(8,128)(2,1)} async-done(((bf16[1,256,4096]{2,1,0:T(8,128)(2,1)}), bf16[1,1024,4096]{2,1,0:T(8,128)(2,1)}) %all-gather.3.cloned.1.call-update) | async-done | bytes 8388624 | tf_op jit(solution)/shard_map/all_gather | solution.py:24
  161.9 15.1 %fusion.6 = f32[1024,1024]{1,0:T(8,128)} fusion(bf16[1024,4096]{1,0:T(8,128)(2,1)} %param.12, bf16[1,1024,4096]{2,1,0:T(8,128)(2,1)} %all-gather.3.cloned.1.call-done), kind=kOutput, calls=%fused_computation.12 | convolution fusion | flops 8589934592 | bytes 20971520 | tf_op jit(solution)/shard_map/dot_general | solution.py:25
  177.2 14.6 %fusion.8 = bf16[1024,4096]{1,0:T(8,128)(2,1)} fusion(bf16[1,1024,4096]{2,1,0:T(8,128)(2,1)} %all-gather.3.cloned.1.call-done, bf16[1,1024,1024]{2,1,0:T(8,128)(2,1)S(1)} %copy-done.9), kind=kOutput, calls=%fused_computation.14 | convolution fusion | flops 8594128896 | bytes 18874368 | tf_op jit(solution)/shard_map/dot_general | solution.py:29
  195.5 1.6 convert_bitcast_fusion
  197.1 1.8 copy.79
  201.1 2.2 gather_fusion
  203.3 2.2 gather_fusion.1
  207.5 9.4 %fusion.3 = (f32[8,512]{1,0:T(8,128)S(1)}, f32[8,1024,512]{2,1,0:T(8,128)}) fusion(pred[512,1024]{0,1:T(8,128)(4,1)S(1)} %fusion.19, bf16[512,8,128]{2,1,0:T(8,128)(2,1)S(1)} %bitcast.109, bf16[8,1024,128]{2,1,0:T(8,128)(2,1)} %gather_fusion, pred[8]{0:T(512)(128)(4,1)S(1)} %compare_and_fusion), kind=kOutput, calls=%fused_computation.9 | convolution fusion | flops 1087369216 | bytes 20463624 | tf_op jit(solution)/shard_map/qhd,khd->hqk/dot_general | solution.py:69
  216.9 9.4 %exponential_reduce_fusion = f32[8,512]{1,0:T(8,128)S(1)} fusion(f32[8,1024,512]{2,1,0:T(8,128)} %get-tuple-element.24, f32[8,512]{1,0:T(8,128)S(1)} %get-tuple-element.23, pred[512,1024]{0,1:T(8,128)(4,1)S(1)} %fusion.19), kind=kLoop, calls=%fused_computation.8 | loop fusion | flops 16773120 | bytes 17334272 | tf_op jit(solution)/shard_map/reduce_sum | solution.py:74
  227.9 1.9 reduce-scatter.5.cloned.1.call-done
  229.7 2.9 convert_bitcast_fusion.1
  234.1 11.7 %multiply_convert_fusion = bf16[8,512,1024]{1,2,0:T(8,128)(2,1)S(1)} fusion(f32[8,1024,512]{2,1,0:T(8,128)} %get-tuple-element.24, f32[8,512]{1,0:T(8,128)S(1)} %copy.58, f32[8,512]{1,0:T(8,128)S(1)} %log_add_fusion, pred[512,1024]{0,1:T(8,128)(4,1)S(1)} %copy-done.4, bf16[8,1024,128]{2,1,0:T(8,128)(2,1)} %gather_fusion.1, ...), kind=kOutput, calls=%fused_computation.7 | convolution fusion | flops 1104150528 | bytes 28868616 | tf_op jit(solution)/shard_map/qhd,khd->hqk/dot_general | solution.py:78
  245.8 3.5 multiply_reduce_fusion
  249.3 4.3 %all-to-all-start = ((f32[4,256,128]{2,1,0:T(8,128)}), f32[4,256,128]{2,1,0:T(8,128)S(1)}, u32[]{:S(2)}, u32[]{:S(2)}) async-start(f32[4,256,128]{2,1,0:T(8,128)} %bitcast.12), calls=%async_computation.1 | async-start | bytes 1048576 | tf_op jit(solution)/shard_map/all_to_all | solution.py:108
  253.7 11.3 %fusion.2 = bf16[1024,512,8]{1,0,2:T(8,128)(2,1)} fusion(f32[8,1024,512]{2,1,0:T(8,128)} %get-tuple-element.24, f32[512,8]{0,1:T(8,128)S(1)} %bitcast.113, pred[1024,512]{1,0:T(8,128)(4,1)S(1)} %fusion.43), kind=kLoop, calls=%fused_computation.5 | loop fusion | flops 20971520 | bytes 25706496 | tf_op jit(solution)/shard_map/convert_element_type | solution.py:76
  265.0 3.0 all-to-all-done
  269.4 6.0 %convolution_bitcast_fusion = f32[4,256,128]{2,1,0:T(8,128)S(1)} fusion(bf16[4,256,512,8]{2,1,0,3:T(8,128)(2,1)} %bitcast.97, bf16[512,8,128,1]{2,1,0,3:T(8,128)(2,1)S(1)} %bitcast.101), kind=kOutput, calls=%fused_computation.32 | convolution fusion | flops 1073741824 | bytes 9961472 | tf_op jit(solution)/shard_map/hqk,qhd->hkd/dot_general | solution.py:77
  275.3 16.5 %all_to_all.29 = f32[4,256,128]{2,1,0:T(8,128)S(1)} all-to-all(f32[4,256,128]{2,1,0:T(8,128)S(1)} %convolution_bitcast_fusion), channel_id=1, replica_groups=mesh['dp'=4,'ctx'=4,'tsp'=2] {'ctx'}, dimensions={0} | all-to-all | bytes 1048576 | tf_op jit(solution)/shard_map/all_to_all | solution.py:109
  292.9 10.9 %reduce-scatter.11.cloned.1.call-done = bf16[256,4096]{1,0:T(8,128)(2,1)} async-done(((bf16[1024,4096]{1,0:T(8,128)(2,1)}), bf16[256,4096]{1,0:T(8,128)(2,1)}) %reduce-scatter.11.cloned.1.call-update) | async-done | bytes 2097168 | tf_op jit(solution)/shard_map/reduce_scatter | solution.py:33
  303.8 5.6 %multiply_convert_fusion.1 = bf16[8,128,512]{2,1,0:T(8,128)(2,1)S(1)} fusion(bf16[8,512,1024]{1,2,0:T(8,128)(2,1)} %copy-done.12, bf16[8,1024,128]{2,1,0:T(8,128)(2,1)} %gather_fusion, pred[8]{0:T(512)(128)(4,1)S(1)} %compare_and_fusion), kind=kOutput, calls=%fused_computation.24 | convolution fusion | flops 1075838976 | bytes 11534344 | tf_op jit(solution)/shard_map/hqk,khd->qhd/dot_general | solution.py:85
  310.7 10.3 %reduce-scatter.7.cloned.1.call-done = f32[128,512]{0,1:T(8,128)} async-done(((f32[256,512]{0,1:T(8,128)}), f32[128,512]{0,1:T(8,128)}) %reduce-scatter.7.cloned.1.call-update) | async-done | bytes 262160 | tf_op jit(solution)/shard_map/reduce_scatter | solution.py:112
  322.8 15.0 %reduce-scatter.9.cloned.1.call-done = f32[128,512]{0,1:T(8,128)} async-done(((f32[256,512]{0,1:T(8,128)}), f32[128,512]{0,1:T(8,128)}) %reduce-scatter.9.cloned.1.call-update) | async-done | bytes 262160 | tf_op jit(solution)/shard_map/reduce_scatter | solution.py:113
  339.5 58.0 %all-gather.5.cloned.1.call-done = bf16[1024,4096]{1,0:T(8,128)(2,1)} async-done(((bf16[256,4096]{1,0:T(8,128)(2,1)}), bf16[1024,4096]{1,0:T(8,128)(2,1)}) %all-gather.5.cloned.1.call-update) | async-done | bytes 8388624 | tf_op jit(solution)/shard_map/all_gather | solution.py:36
  397.5 11.8 %convert_element_type.48 = f32[1024,4096]{1,0:T(8,128)} convert(bf16[1024,4096]{1,0:T(8,128)(2,1)} %all-gather.5.cloned.1.call-done) | non-fusion elementwise | flops 4194304 | bytes 25165824 | tf_op jit(solution)/shard_map/convert_element_type | solution.py:36
  (66 shorter events, 18.9 us)
Async XLA Ops:
  7.2 154.7 %all-gather.3.cloned.1.call-start = ((), (), s32[]{:S(2)}) async-start(), calls=%async_computation.6 | async-start | bytes 10485760 | tf_op jit(solution)/shard_map/all_gather | solution.py:24
  7.9 169.3 %copy-start.9 = (bf16[1,1024,1024]{2,1,0:T(8,128)(2,1)S(1)}, bf16[1,1024,1024]{2,1,0:T(8,128)(2,1)}, u32[]{:S(2)}) copy-start(bf16[1,1024,1024]{2,1,0:T(8,128)(2,1)} %param.11) | copy-start | bytes 6291460
  7.9 221.8 %reduce-scatter.5.cloned.1.call-start = ((), (), s32[]{:S(2)}) async-start(), calls=%async_computation.7 | async-start | bytes 6291456 | tf_op jit(solution)/shard_map/reduce_scatter | solution.py:37
  177.0 126.7 %reduce-scatter.11.cloned.1.call-start = ((), (), s32[]{:S(2)}) async-start(), calls=%async_computation.10 | async-start | bytes 10485760 | tf_op jit(solution)/shard_map/reduce_scatter | solution.py:33
  191.8 0.7 copy-start.11
  191.8 1.2 copy-start.5
  191.8 2.5 copy-start.6
  197.1 8.4 %copy-start.10 = (s32[1,1024]{1,0:T(1,128)S(1)}, s32[1,1024]{1,0:T(1,128)}, u32[]{:S(2)}) copy-start(s32[1,1024]{1,0:T(1,128)} %param.16) | copy-start | bytes 12292
  201.1 6.4 %copy-start.7 = (bf16[64,8,8,128]{3,2,1,0:T(8,128)(2,1)S(1)}, bf16[64,8,8,128]{3,2,1,0:T(8,128)(2,1)}, u32[]{:S(2)}) copy-start(bf16[64,8,8,128]{3,2,1,0:T(8,128)(2,1)} %copy.77) | copy-start | bytes 3145732
  207.4 9.4 %copy-start.3 = (pred[512,1024]{0,1:T(8,128)(4,1)}, pred[512,1024]{0,1:T(8,128)(4,1)S(1)}, u32[]{:S(2)}) copy-start(pred[512,1024]{0,1:T(8,128)(4,1)S(1)} %fusion.19) | copy-start | bytes 1572868
  216.9 16.0 %copy-start = (f32[64,8,8,128]{3,2,1,0:T(8,128)S(1)}, f32[64,8,8,128]{3,2,1,0:T(8,128)}, u32[]{:S(2)}) copy-start(f32[64,8,8,128]{3,2,1,0:T(8,128)} %copy.79) | copy-start | bytes 6291460
  227.9 6.2 %copy-start.4 = (pred[512,1024]{0,1:T(8,128)(4,1)S(1)}, pred[512,1024]{0,1:T(8,128)(4,1)}, u32[]{:S(2)}) copy-start(pred[512,1024]{0,1:T(8,128)(4,1)} %copy-done.3) | copy-start | bytes 1572868
  232.9 1.0 copy-start.1
  234.0 11.7 %copy-start.8 = (bf16[64,8,8,128]{3,2,1,0:T(8,128)(2,1)S(1)}, bf16[64,8,8,128]{3,2,1,0:T(8,128)(2,1)}, u32[]{:S(2)}) copy-start(bf16[64,8,8,128]{3,2,1,0:T(8,128)(2,1)} %copy.77) | copy-start | bytes 3145732
  245.8 3.6 copy-start.12
  249.3 18.7 %all-to-all-start = ((f32[4,256,128]{2,1,0:T(8,128)}), f32[4,256,128]{2,1,0:T(8,128)S(1)}, u32[]{:S(2)}, u32[]{:S(2)}) async-start(f32[4,256,128]{2,1,0:T(8,128)} %bitcast.12), calls=%async_computation.1 | async-start | bytes 1048576 | tf_op jit(solution)/shard_map/all_to_all | solution.py:108
  253.7 67.4 %reduce-scatter.7.cloned.1.call-start = ((), (), s32[]{:S(2)}) async-start(), calls=%async_computation.8 | async-start | bytes 786432 | tf_op jit(solution)/shard_map/reduce_scatter | solution.py:112
  253.7 15.7 %copy-start.2 = (bf16[64,8,8,128]{3,2,1,0:T(8,128)(2,1)S(1)}, bf16[64,8,8,128]{3,2,1,0:T(8,128)(2,1)}, u32[]{:S(2)}) copy-start(bf16[64,8,8,128]{3,2,1,0:T(8,128)(2,1)} %copy-done.1) | copy-start | bytes 3145732
  269.0 68.8 %reduce-scatter.9.cloned.1.call-start = ((), (), s32[]{:S(2)}) async-start(), calls=%async_computation.9 | async-start | bytes 786432 | tf_op jit(solution)/shard_map/reduce_scatter | solution.py:113
  292.8 104.7 %all-gather.5.cloned.1.call-start = ((), (), s32[]{:S(2)}) async-start(), calls=%async_computation.11 | async-start | bytes 10485760 | tf_op jit(solution)/shard_map/all_gather | solution.py:36
Sparse Core Ops, SparseCore 0:
  9.5 152.3 all-gather.2
  177.1 52.5 reduce-scatter.4
  232.3 71.3 reduce-scatter.10
  306.4 14.6 reduce-scatter.6
  323.1 14.6 reduce-scatter.8
  339.2 58.2 all-gather.4
where the time goes:
time: 417 us; the launch traced here: 416 us
  waiting for transfers between devices  254 us (61%)
  matrix products  65.9 us (16%)
  other arithmetic  42.8 us (10%)
  local copies, waits for them, and re-layouts  17.9 us (4%)
  blocking collectives  16.5 us (4%)
  between operations  14.4 us (3%)
  starting transfers between devices  4.98 us (1%)
    all_gather x1, waiting for transfers between devices, per_device(): dy_block = lax.all_gather(grad_out, 'ctx', axis=1, tiled=True)[0]  154 us
    all_gather x1, waiting for transfers between devices, per_device(): lax.all_gather(weight_quarter, 'dp', axis=0, tiled=True).astype(jnp.float32)  58 us
    all_to_all x1, blocking collectives, per_device(): lax.all_to_all(fold_local(value_terms), 'ctx', split_axis=0, concat_axis=...  16.5 us
    dot_general x1, matrix products, per_device(): lax.dot_general(dy_block, out_weight, (((1,), (1,)), ((), ())), preferred...  15.1 us
    reduce_scatter x1, waiting for transfers between devices, per_device(): lax.psum_scatter(fold_remote(value_recv), 'tsp', scatter_dimension=0, til...  15 us
    dot_general x1, matrix products, per_device(): lax.dot_general(out_all, dy_block, (((0,), (0,)), ((), ())), preferred_el...  14.6 us
    convert_element_type x1, other arithmetic, per_device(): lax.all_gather(weight_quarter, 'dp', axis=0, tiled=True).astype(jnp.float32)  11.8 us
    dot_general x1, matrix products, per_device(): jnp.einsum('qhd,khd->hqk', grad_heads, value_heads, preferred_element_typ...  11.7 us
  transfers between devices with their start and end apart: 7, of which 7 were waited for; matrix products, arithmetic and copies ran while one was open for 24% of the time, Pallas kernels for 0%

commit v1 on v0

--- a/solution.py
+++ b/solution.py
@@ -106,8 +106,11 @@
         return folded.reshape(recv.shape[0], KV_HEADS * HEAD_DIM)
 
     key_recv = lax.all_to_all(fold_local(key_terms), "ctx", split_axis=0, concat_axis=1, tiled=True)
-    value_recv = lax.all_to_all(
-        fold_local(value_terms), "ctx", split_axis=0, concat_axis=1, tiled=True
+    value_recv = jnp.concatenate(
+        lax.all_to_all(
+            jnp.stack(jnp.split(fold_local(value_terms), lax.axis_size("ctx"), axis=0)), "ctx", 0, 0
+        ),
+        axis=1,
     )
     key_part = lax.psum_scatter(fold_remote(key_recv), "tsp", scatter_dimension=0, tiled=True)
     value_part = lax.psum_scatter(fold_remote(value_recv), "tsp", scatter_dimension=0, tiled=True)

time: 417 us -> 417 us (level)
  other arithmetic: 42.8 us -> 30 us
  waiting for transfers between devices: 254 us -> 265 us
    convert_element_type x1 -> x0, other arithmetic: 11.3 us -> none  [per_device(): probs = probs_f.astype(jnp.bfloat16)]
    reduce_scatter x1, waiting for transfers between devices: 10.9 us -> 17.3 us  [per_device(): lax.psum_scatter(weight_part.astype(jnp.bfloat16), 'dp', scatter_dimensio...]
    unnamed x34 -> x30, local copies, waits for them, and re-layouts: 9.7 us -> 9.51 us
  transfers between devices with their start and end apart: 7 -> 7, of which waited for: 7 -> 7; matrix products, arithmetic and copies ran while one was open for 24% -> 21% of each run, Pallas kernels for 0% -> 0%
where the time goes in v1:
time: 417 us; the launch traced here: 416 us
  waiting for transfers between devices  265 us (64%)
  matrix products  67.2 us (16%)
  other arithmetic  30 us (7%)
  local copies, waits for them, and re-layouts  17.7 us (4%)
  blocking collectives  16.4 us (4%)
  between operations  14.4 us (3%)
  starting transfers between devices  5.14 us (1%)
    all_gather x1, waiting for transfers between devices, per_device(): dy_block = lax.all_gather(grad_out, 'ctx', axis=1, tiled=True)[0]  154 us
    all_gather x1, waiting for transfers between devices, per_device(): lax.all_gather(weight_quarter, 'dp', axis=0, tiled=True).astype(jnp.float32)  58 us
    reduce_scatter x1, waiting for transfers between devices, per_device(): lax.psum_scatter(weight_part.astype(jnp.bfloat16), 'dp', scatter_dimensio...  17.3 us
    all_to_all x1, blocking collectives, per_device(): lax.all_to_all(jnp.stack(jnp.split(fold_local(value_terms), lax.axis_size...  16.4 us
    dot_general x1, matrix products, per_device(): lax.dot_general(dy_block, out_weight, (((1,), (1,)), ((), ())), preferred...  15.1 us
    reduce_scatter x1, waiting for transfers between devices, per_device(): lax.psum_scatter(fold_remote(value_recv), 'tsp', scatter_dimension=0, til...  15 us
    dot_general x1, matrix products, per_device(): lax.dot_general(out_all, dy_block, (((0,), (0,)), ((), ())), preferred_el...  14.6 us
    convert_element_type x1, other arithmetic, per_device(): lax.all_gather(weight_quarter, 'dp', axis=0, tiled=True).astype(jnp.float32)  11.8 us
  transfers between devices with their start and end apart: 7, of which 7 were waited for; matrix products, arithmetic and copies ran while one was open for 21% of the time, Pallas kernels for 0%

profile of v1, /device:TPU:0, one launch (start us, length us, event | category | flops | bytes accessed | tf_op | source)
XLA Modules:
  0.0 416.2 jit_solution(12407456058514520362)
XLA Ops:
  8.0 154.0 %all-gather.3.cloned.1.call-done = bf16[1,1024,4096]{2,1,0:T(8,128)(2,1)} async-done(((bf16[1,256,4096]{2,1,0:T(8,128)(2,1)}), bf16[1,1024,4096]{2,1,0:T(8,128)(2,1)}) %all-gather.3.cloned.1.call-update) | async-done | bytes 8388624 | tf_op jit(solution)/shard_map/all_gather | solution.py:24
  161.9 15.1 %fusion.4 = f32[1024,1024]{1,0:T(8,128)} fusion(bf16[1024,4096]{1,0:T(8,128)(2,1)} %param.12, bf16[1,1024,4096]{2,1,0:T(8,128)(2,1)} %all-gather.3.cloned.1.call-done), kind=kOutput, calls=%fused_computation.10 | convolution fusion | flops 8589934592 | bytes 20971520 | tf_op jit(solution)/shard_map/dot_general | solution.py:25
  177.2 14.6 %fusion.9 = bf16[1024,4096]{1,0:T(8,128)(2,1)} fusion(bf16[1,1024,4096]{2,1,0:T(8,128)(2,1)} %all-gather.3.cloned.1.call-done, bf16[1,1024,1024]{2,1,0:T(8,128)(2,1)S(1)} %copy-done.7), kind=kOutput, calls=%fused_computation.14 | convolution fusion | flops 8594128896 | bytes 18874368 | tf_op jit(solution)/shard_map/dot_general | solution.py:29
  195.5 1.6 convert_bitcast_fusion
  197.1 1.8 copy.74
  201.2 2.2 gather_fusion
  203.3 2.1 gather_fusion.1
  205.9 1.5 fusion.20
  207.5 9.2 %fusion.1 = (f32[8,512]{1,0:T(8,128)S(1)}, f32[8,1024,512]{2,1,0:T(8,128)}) fusion(pred[512,1024]{0,1:T(8,128)(4,1)S(1)} %fusion.20, bf16[512,8,128]{2,1,0:T(8,128)(2,1)S(1)} %bitcast.97, bf16[8,1024,128]{2,1,0:T(8,128)(2,1)} %gather_fusion, pred[8]{0:T(512)(128)(4,1)S(1)} %compare_and_fusion), kind=kOutput, calls=%fused_computation.7 | convolution fusion | flops 1087369216 | bytes 20463624 | tf_op jit(solution)/shard_map/qhd,khd->hqk/dot_general | solution.py:69
  216.7 9.4 %exponential_reduce_fusion = f32[8,512]{1,0:T(8,128)S(1)} fusion(f32[8,1024,512]{2,1,0:T(8,128)} %get-tuple-element.28, f32[8,512]{1,0:T(8,128)S(1)} %get-tuple-element.27, pred[512,1024]{0,1:T(8,128)(4,1)S(1)} %fusion.20), kind=kLoop, calls=%fused_computation.5 | loop fusion | flops 16773120 | bytes 17334272 | tf_op jit(solution)/shard_map/reduce_sum | solution.py:74
  226.1 3.6 reduce-scatter.5.cloned.1.call-done
  229.7 2.9 convert_bitcast_fusion.1
  233.7 11.3 %multiply_convert_fusion = bf16[8,512,1024]{1,2,0:T(8,128)(2,1)S(1)} fusion(f32[8,1024,512]{2,1,0:T(8,128)} %get-tuple-element.28, f32[8,512]{1,0:T(8,128)S(1)} %copy.56, f32[8,512]{1,0:T(8,128)S(1)} %log_add_fusion, pred[512,1024]{0,1:T(8,128)(4,1)S(1)} %fusion.20, bf16[8,1024,128]{2,1,0:T(8,128)(2,1)} %gather_fusion.1, ...), kind=kOutput, calls=%fused_computation.3 | convolution fusion | flops 1104150528 | bytes 28868616 | tf_op jit(solution)/shard_map/qhd,khd->hqk/dot_general | solution.py:78
  245.0 3.5 multiply_reduce_fusion
  248.7 4.5 %all-to-all-start = ((f32[4,256,128]{2,1,0:T(8,128)}), f32[4,256,128]{2,1,0:T(8,128)S(1)}, u32[]{:S(2)}, u32[]{:S(2)}) async-start(f32[4,256,128]{2,1,0:T(8,128)} %bitcast.12), calls=%async_computation.1 | async-start | bytes 1048576 | tf_op jit(solution)/shard_map/all_to_all | solution.py:108
  253.2 8.5 %fusion.24 = f32[1,1024,128]{2,1,0:T(8,128)S(1)} fusion(f32[8,1024,512]{2,1,0:T(8,128)} %get-tuple-element.28, f32[8,512]{1,0:T(8,128)S(1)} %log_add_fusion, pred[512,1024]{0,1:T(8,128)(4,1)S(1)} %fusion.20, bf16[64,8,8,128]{3,2,1,0:T(8,128)(2,1)S(1)} %copy-done.6), kind=kOutput, calls=%fused_computation.32 | convolution fusion | flops 1094713344 | bytes 18890752 | tf_op jit(solution)/shard_map/hqk,qhd->hkd/dot_general | solution.py:77
  261.7 5.8 %all-to-all-done = f32[4,256,128]{2,1,0:T(8,128)S(1)} async-done(((f32[4,256,128]{2,1,0:T(8,128)}), f32[4,256,128]{2,1,0:T(8,128)S(1)}, u32[]{:S(2)}, u32[]{:S(2)}) %all-to-all-start) | async-done | bytes 524320 | tf_op jit(solution)/shard_map/all_to_all | solution.py:108
  268.9 16.4 %all_to_all.21 = f32[4,256,128]{2,1,0:T(8,128)S(1)} all-to-all(f32[4,256,128]{2,1,0:T(8,128)S(1)} %pad_maximum_fusion), channel_id=1, replica_groups=mesh['dp'=4,'ctx'=4,'tsp'=2] {'ctx'}, dimensions={0} | all-to-all | bytes 1048576 | tf_op jit(solution)/shard_map/all_to_all | solution.py:110
  286.5 17.3 %reduce-scatter.11.cloned.1.call-done = bf16[256,4096]{1,0:T(8,128)(2,1)} async-done(((bf16[1024,4096]{1,0:T(8,128)(2,1)}), bf16[256,4096]{1,0:T(8,128)(2,1)}) %reduce-scatter.11.cloned.1.call-update) | async-done | bytes 2097168 | tf_op jit(solution)/shard_map/reduce_scatter | solution.py:33
  303.8 5.0 %multiply_convert_fusion.1 = bf16[8,128,512]{2,1,0:T(8,128)(2,1)S(1)} fusion(bf16[8,512,1024]{1,2,0:T(8,128)(2,1)} %copy-done.10, bf16[8,1024,128]{2,1,0:T(8,128)(2,1)S(1)} %copy-done.1, pred[8]{0:T(512)(128)(4,1)S(1)} %compare_and_fusion), kind=kOutput, calls=%fused_computation.24 | convolution fusion | flops 1075838976 | bytes 11534344 | tf_op jit(solution)/shard_map/hqk,khd->qhd/dot_general | solution.py:85
  310.1 11.0 %reduce-scatter.7.cloned.1.call-done = f32[128,512]{0,1:T(8,128)} async-done(((f32[256,512]{0,1:T(8,128)}), f32[128,512]{0,1:T(8,128)}) %reduce-scatter.7.cloned.1.call-update) | async-done | bytes 262160 | tf_op jit(solution)/shard_map/reduce_scatter | solution.py:115
  322.8 15.0 %reduce-scatter.9.cloned.1.call-done = f32[128,512]{0,1:T(8,128)} async-done(((f32[256,512]{0,1:T(8,128)}), f32[128,512]{0,1:T(8,128)}) %reduce-scatter.9.cloned.1.call-update) | async-done | bytes 262160 | tf_op jit(solution)/shard_map/reduce_scatter | solution.py:116
  339.6 58.0 %all-gather.5.cloned.1.call-done = bf16[1024,4096]{1,0:T(8,128)(2,1)} async-done(((bf16[256,4096]{1,0:T(8,128)(2,1)}), bf16[1024,4096]{1,0:T(8,128)(2,1)}) %all-gather.5.cloned.1.call-update) | async-done | bytes 8388624 | tf_op jit(solution)/shard_map/all_gather | solution.py:36
  397.6 11.8 %convert_element_type.47 = f32[1024,4096]{1,0:T(8,128)} convert(bf16[1024,4096]{1,0:T(8,128)(2,1)} %all-gather.5.cloned.1.call-done) | non-fusion elementwise | flops 4194304 | bytes 25165824 | tf_op jit(solution)/shard_map/convert_element_type | solution.py:36
  (62 shorter events, 15.7 us)
Async XLA Ops:
  7.2 154.7 %all-gather.3.cloned.1.call-start = ((), (), s32[]{:S(2)}) async-start(), calls=%async_computation.6 | async-start | bytes 10485760 | tf_op jit(solution)/shard_map/all_gather | solution.py:24
  7.9 169.3 %copy-start.7 = (bf16[1,1024,1024]{2,1,0:T(8,128)(2,1)S(1)}, bf16[1,1024,1024]{2,1,0:T(8,128)(2,1)}, u32[]{:S(2)}) copy-start(bf16[1,1024,1024]{2,1,0:T(8,128)(2,1)} %param.11) | copy-start | bytes 6291460
  7.9 221.8 %reduce-scatter.5.cloned.1.call-start = ((), (), s32[]{:S(2)}) async-start(), calls=%async_computation.7 | async-start | bytes 6291456 | tf_op jit(solution)/shard_map/reduce_scatter | solution.py:37
  177.0 126.8 %reduce-scatter.11.cloned.1.call-start = ((), (), s32[]{:S(2)}) async-start(), calls=%async_computation.10 | async-start | bytes 10485760 | tf_op jit(solution)/shard_map/reduce_scatter | solution.py:33
  191.8 0.7 copy-start.9
  191.8 1.2 copy-start.2
  191.8 2.5 copy-start.3
  197.1 8.4 %copy-start.8 = (s32[1,1024]{1,0:T(1,128)S(1)}, s32[1,1024]{1,0:T(1,128)}, u32[]{:S(2)}) copy-start(s32[1,1024]{1,0:T(1,128)} %param.16) | copy-start | bytes 12292
  201.1 6.3 %copy-start.4 = (bf16[64,8,8,128]{3,2,1,0:T(8,128)(2,1)S(1)}, bf16[64,8,8,128]{3,2,1,0:T(8,128)(2,1)}, u32[]{:S(2)}) copy-start(bf16[64,8,8,128]{3,2,1,0:T(8,128)(2,1)} %copy.72) | copy-start | bytes 3145732
  216.7 16.2 %copy-start = (f32[64,8,8,128]{3,2,1,0:T(8,128)S(1)}, f32[64,8,8,128]{3,2,1,0:T(8,128)}, u32[]{:S(2)}) copy-start(f32[64,8,8,128]{3,2,1,0:T(8,128)} %copy.74) | copy-start | bytes 6291460
  233.7 11.3 %copy-start.5 = (bf16[64,8,8,128]{3,2,1,0:T(8,128)(2,1)S(1)}, bf16[64,8,8,128]{3,2,1,0:T(8,128)(2,1)}, u32[]{:S(2)}) copy-start(bf16[64,8,8,128]{3,2,1,0:T(8,128)(2,1)} %copy.72) | copy-start | bytes 3145732
  245.0 3.7 copy-start.10
  245.0 8.2 %copy-start.6 = (bf16[64,8,8,128]{3,2,1,0:T(8,128)(2,1)S(1)}, bf16[64,8,8,128]{3,2,1,0:T(8,128)(2,1)}, u32[]{:S(2)}) copy-start(bf16[64,8,8,128]{3,2,1,0:T(8,128)(2,1)} %get-tuple-element.21) | copy-start | bytes 3145732
  248.7 18.8 %all-to-all-start = ((f32[4,256,128]{2,1,0:T(8,128)}), f32[4,256,128]{2,1,0:T(8,128)S(1)}, u32[]{:S(2)}, u32[]{:S(2)}) async-start(f32[4,256,128]{2,1,0:T(8,128)} %bitcast.12), calls=%async_computation.1 | async-start | bytes 1048576 | tf_op jit(solution)/shard_map/all_to_all | solution.py:108
  253.2 67.9 %reduce-scatter.7.cloned.1.call-start = ((), (), s32[]{:S(2)}) async-start(), calls=%async_computation.8 | async-start | bytes 786432 | tf_op jit(solution)/shard_map/reduce_scatter | solution.py:115
  261.7 42.1 %copy-start.1 = (bf16[8,1024,128]{2,1,0:T(8,128)(2,1)S(1)}, bf16[8,1024,128]{2,1,0:T(8,128)(2,1)}, u32[]{:S(2)}) copy-start(bf16[8,1024,128]{2,1,0:T(8,128)(2,1)} %gather_fusion) | copy-start | bytes 6291460
  268.5 69.3 %reduce-scatter.9.cloned.1.call-start = ((), (), s32[]{:S(2)}) async-start(), calls=%async_computation.9 | async-start | bytes 786432 | tf_op jit(solution)/shard_map/reduce_scatter | solution.py:116
  286.4 111.1 %all-gather.5.cloned.1.call-start = ((), (), s32[]{:S(2)}) async-start(), calls=%async_computation.11 | async-start | bytes 10485760 | tf_op jit(solution)/shard_map/all_gather | solution.py:36
Sparse Core Ops, SparseCore 0:
  9.5 152.3 all-gather.2
  177.1 52.5 reduce-scatter.4
  232.3 71.4 reduce-scatter.10
  306.4 14.6 reduce-scatter.6
  323.2 14.6 reduce-scatter.8
  339.2 58.2 all-gather.4
